TPU v7x, 256 devices: a whole 4x4x8 slice. The times are simulated.
256 devices in a mesh: row: 8 (over z_hi, core), col: 32 (over z_lo, x, y).
Axes of the slice: x: 4, y: 4, z: 8 (z_hi: 4, z_lo: 2; z = z_hi * 2 + z_lo), core: 2. Of those that a mesh axis runs over, the one named last changes fastest.
Arguments:
- panel_adj: float32 [14336, 512], P('row', 'col'), may hold values from -6 to 6
- inv_diag: float32 [512, 512], P('col'), may hold values from -0.25 to 0.25
- row_panel: float32 [512, 14336], P('row', 'col'), may hold values from -0.25 to 0.25
- trailing_adj: float32 [14336, 14336], P('row', 'col'), may hold values from -6 to 6
- trailing_factor: float32 [14336, 14336], P('row', 'col'), may hold values from -0.046875 to 0.046875
Outputs:
- trailing_new: float32 [14336, 14336], P('row', 'col')
- row_adj: float32 [512, 14336], P('row', 'col')
All inputs are finite; a program needn't handle non-finite values.
Results may differ from a plain program's by a relative error of at most 0.00007.
Values sent between devices are 32-bit elements; how exact they have to be, the bound alone decides.
A program may use at most 64 MiB of HBM per device.

v0:
```python
import jax
import jax.numpy as jnp
from jax import lax
from jax.sharding import PartitionSpec as P


def local(panel_adj, inv_diag, row_panel, trailing_adj, trailing_factor):
    highest = lax.Precision.HIGHEST
    inverse_all = lax.all_gather(inv_diag, "col", axis=0, tiled=True)
    scaled = jnp.dot(
        lax.all_gather(panel_adj, "col", axis=1, tiled=True),
        inverse_all,
        precision=highest,
        preferred_element_type=jnp.float32,
    )
    trailing_new = trailing_adj - jnp.dot(
        scaled,
        lax.all_gather(row_panel, "row", axis=0, tiled=True),
        precision=highest,
        preferred_element_type=jnp.float32,
    )
    terms_local = lax.dot_general(
        scaled,
        trailing_factor,
        (((0,), (0,)), ((), ())),
        precision=highest,
        preferred_element_type=jnp.float32,
    )
    row_adj = lax.psum_scatter(terms_local, "row", scatter_dimension=0, tiled=True)
    return (trailing_new, row_adj)


def solution(mesh):
    placed = (P("row", "col"), P("col", None), P("row", "col"), P("row", "col"), P("row", "col"))
    return jax.shard_map(
        local,
        mesh=mesh,
        in_specs=placed,
        out_specs=(P("row", "col"), P("row", "col")),
        check_vma=False,
    )
```

profile of v0, /device:TPU:8, one launch (start us, length us, event | category | flops | bytes accessed | tf_op | source)
XLA Modules:
  0.0 397.3 jit_solution(17460314961301271969)
XLA Ops:
  7.2 0.0 copy-start
  7.2 0.0 all-gather.5.cloned.1.call-start
  7.2 0.7 all-gather.5.cloned.1.call-update
  7.9 0.0 all-gather.3.cloned.1.call-start
  8.0 0.7 all-gather.3.cloned.1.call-update
  8.7 0.0 reduce-scatter.2.cloned.1.call-start
  8.7 157.2 %all-gather.5.cloned.1.call-done = f32[512,512]{1,0:T(8,128)} async-done(((f32[16,512]{1,0:T(8,128)}), f32[512,512]{1,0:T(8,128)}) %all-gather.5.cloned.1.call-update) | async-done | bytes 1048592 | tf_op jit(solution)/shard_map/all_gather | solution.py:9
  165.9 160.2 %all-gather.3.cloned.1.call-done = f32[1792,512]{0,1:T(8,128)} async-done(((f32[1792,16]{0,1:T(8,128)}), f32[1792,512]{0,1:T(8,128)}) %all-gather.3.cloned.1.call-update) | async-done | bytes 3670032 | tf_op jit(solution)/shard_map/all_gather | solution.py:11
  326.1 8.5 %fusion = f32[1792,512]{1,0:T(8,128)S(1)} fusion(f32[1792,512]{0,1:T(8,128)} %all-gather.3.cloned.1.call-done, f32[512,512]{1,0:T(8,128)} %all-gather.5.cloned.1.call-done), kind=kOutput, calls=%fused_computation.1 | convolution fusion | flops 5637144576 | bytes 8388608 | tf_op jit(solution)/shard_map/dot_general | solution.py:10
  334.6 0.0 copy-start.1
  334.7 1.8 copy-done.1
  336.4 0.0 copy-done
  336.4 0.0 copy-start.2
  336.4 13.0 %fusion.1 = f32[512,448]{1,0:T(8,128)} fusion(f32[1792,512]{1,0:T(8,128)S(1)} %fusion, f32[1792,448]{0,1:T(8,128)S(1)} %copy-done), kind=kOutput, calls=%fused_computation.2 | convolution fusion | flops 4932501504 | bytes 7798784 | tf_op jit(solution)/shard_map/dot_general | solution.py:22
  349.4 0.0 reduce-scatter.2.cloned.1.call-update
  349.5 0.0 copy-done.2
  349.5 20.0 %all_gather.11 = f32[512,448]{1,0:T(8,128)S(1)} all-gather(f32[64,448]{1,0:T(8,128)S(1)} %copy-done.2), channel_id=1, replica_groups=mesh['row'=8,'col'=32] {'row'}, dimensions={0}, use_global_device_ids=true | all-gather | bytes 1032192 | tf_op jit(solution)/shard_map/all_gather | solution.py:18
  369.4 10.4 %convolution_subtract_fusion = f32[1792,448]{0,1:T(8,128)} fusion(f32[1792,448]{0,1:T(8,128)} %param.8, f32[1792,512]{1,0:T(8,128)} %copy-done.1, f32[512,448]{1,0:T(8,128)S(1)} %all_gather.11), kind=kOutput, calls=%fused_computation | convolution fusion | flops 4933304320 | bytes 11010048 | tf_op jit(solution)/shard_map/dot_general | solution.py:16
  379.8 11.0 %reduce-scatter.2.cloned.1.call-done = f32[64,448]{1,0:T(8,128)} async-done(((f32[512,448]{1,0:T(8,128)}), f32[64,448]{1,0:T(8,128)}) %reduce-scatter.2.cloned.1.call-update) | async-done | bytes 114704 | tf_op jit(solution)/shard_map/reduce_scatter | solution.py:29
Async XLA Ops:
  7.2 329.3 %copy-start = (f32[1792,448]{0,1:T(8,128)S(1)}, f32[1792,448]{0,1:T(8,128)}, u32[]{:S(2)}) copy-start(f32[1792,448]{0,1:T(8,128)} %param.9) | copy-start | bytes 9633796
  7.2 158.7 %all-gather.5.cloned.1.call-start = ((), (), s32[]{:S(2)}) async-start(), calls=%async_computation.2 | async-start | bytes 1081344 | tf_op jit(solution)/shard_map/all_gather | solution.py:9
  7.9 318.2 %all-gather.3.cloned.1.call-start = ((), (), s32[]{:S(2)}) async-start(), calls=%async_computation.1 | async-start | bytes 3784704 | tf_op jit(solution)/shard_map/all_gather | solution.py:11
  8.7 382.1 %reduce-scatter.2.cloned.1.call-start = ((), (), s32[]{:S(2)}) async-start(), calls=%async_computation.3 | async-start | bytes 1179648 | tf_op jit(solution)/shard_map/reduce_scatter | solution.py:29
  334.6 1.8 copy-start.1
  336.4 13.0 %copy-start.2 = (f32[64,448]{1,0:T(8,128)S(1)}, f32[64,448]{1,0:T(8,128)}, u32[]{:S(2)}) copy-start(f32[64,448]{1,0:T(8,128)} %param.7) | copy-start | bytes 344068
Sparse Core Ops, SparseCore 0:
  9.8 156.0 all-gather.4
  167.6 158.3 all-gather.2
  349.6 41.1 reduce-scatter.1
where the time goes:
time: 397 us
  waiting for transfers between devices  330 us (83%)
  matrix products  31.9 us (8%)
  blocking collectives  20 us (5%)
  between operations  13.8 us (3%)
    all_gather x1, waiting for transfers between devices, local(): lax.all_gather(panel_adj, 'col', axis=1, tiled=True)  160 us
    all_gather x1, waiting for transfers between devices, local(): inverse_all = lax.all_gather(inv_diag, 'col', axis=0, tiled=True)  157 us
    all_gather x1, blocking collectives, local(): lax.all_gather(row_panel, 'row', axis=0, tiled=True)  20 us
    dot_general x1, matrix products, local(): lax.dot_general(scaled, trailing_factor, (((0,), (0,)), ((), ())), precis...  13 us
    reduce_scatter x1, waiting for transfers between devices, local(): lax.psum_scatter(terms_local, 'row', scatter_dimension=0, tiled=True)  11 us
    dot_general x1, matrix products, local(): jnp.dot(scaled, lax.all_gather(row_panel, 'row', axis=0, tiled=True), pre...  10.4 us
    dot_general x1, matrix products, local(): jnp.dot(lax.all_gather(panel_adj, 'col', axis=1, tiled=True), inverse_all...  8.55 us
  transfers between devices with their start and end apart: 3, of which 3 were waited for; matrix products, arithmetic and copies ran while one was open for 3% of the time, Pallas kernels for 0%

commit v1 on v0

--- a/solution.py
+++ b/solution.py
@@ -6,7 +6,9 @@
 
 def local(panel_adj, inv_diag, row_panel, trailing_adj, trailing_factor):
     highest = lax.Precision.HIGHEST
-    inverse_all = lax.all_gather(inv_diag, "col", axis=0, tiled=True)
+    inverse_all = jnp.concatenate(
+        lax.all_to_all(jnp.stack([inv_diag] * lax.axis_size("col")), "col", 0, 0), axis=0
+    )
     scaled = jnp.dot(
         lax.all_gather(panel_adj, "col", axis=1, tiled=True),
         inverse_all,

time: 397 us -> 245 us (0.62)
  waiting for transfers between devices: 330 us -> 149 us
  blocking collectives: 20 us -> 45.1 us
    all_gather x1 -> x0, waiting for transfers between devices: 157 us -> none  [local(): inverse_all = lax.all_gather(inv_diag, 'col', axis=0, tiled=True)]
    all_to_all x0 -> x1, blocking collectives: none -> 24.8 us  [local(): lax.all_to_all(jnp.stack([inv_diag] * lax.axis_size('col')), 'col', 0, 0)]
    all_gather x1, waiting for transfers between devices: 160 us -> 138 us  [local(): lax.all_gather(panel_adj, 'col', axis=1, tiled=True)]
  transfers between devices with their start and end apart: 3 -> 2, of which waited for: 3 -> 2; matrix products, arithmetic and copies ran while one was open for 3% -> 5% of each run, Pallas kernels for 0% -> 0%
where the time goes in v1:
time: 245 us; the launch traced here: 243 us
  waiting for transfers between devices  149 us (61%)
  blocking collectives  45.1 us (18%)
  matrix products  31.9 us (13%)
  between operations  14.1 us (6%)
  local copies, waits for them, and re-layouts  2.84 us (1%)
    all_gather x1, waiting for transfers between devices, local(): lax.all_gather(panel_adj, 'col', axis=1, tiled=True)  138 us
    all_to_all x1, blocking collectives, local(): lax.all_to_all(jnp.stack([inv_diag] * lax.axis_size('col')), 'col', 0, 0)  24.8 us
    all_gather x1, blocking collectives, local(): lax.all_gather(row_panel, 'row', axis=0, tiled=True)  20.2 us
    dot_general x1, matrix products, local(): lax.dot_general(scaled, trailing_factor, (((0,), (0,)), ((), ())), precis...  13 us
    reduce_scatter x1, waiting for transfers between devices, local(): lax.psum_scatter(terms_local, 'row', scatter_dimension=0, tiled=True)  10.7 us
    dot_general x1, matrix products, local(): jnp.dot(scaled, lax.all_gather(row_panel, 'row', axis=0, tiled=True), pre...  10.4 us
    dot_general x1, matrix products, local(): jnp.dot(lax.all_gather(panel_adj, 'col', axis=1, tiled=True), inverse_all...  8.54 us
  transfers between devices with their start and end apart: 2, of which 2 were waited for; matrix products, arithmetic and copies ran while one was open for 5% of the time, Pallas kernels for 0%

profile of v1, /device:TPU:8, one launch (start us, length us, event | category | flops | bytes accessed | tf_op | source)
XLA Modules:
  0.0 243.2 jit_solution(8438750449241671709)
XLA Ops:
  7.2 0.0 copy-start
  7.2 0.0 all-gather.2.cloned.1.call-start
  7.2 0.7 all-gather.2.cloned.1.call-update
  7.9 0.0 reduce-scatter.2.cloned.1.call-start
  8.0 1.0 stack.2
  9.0 24.8 %all_to_all.5 = f32[32,16,512]{2,1,0:T(8,128)} all-to-all(f32[32,16,512]{2,1,0:T(8,128)S(1)} %stack.2), channel_id=1, replica_groups=mesh['row'=8,'col'=32] {'col'}, dimensions={0} | all-to-all | bytes 2097152 | tf_op jit(solution)/shard_map/all_to_all | solution.py:10
  33.8 137.9 %all-gather.2.cloned.1.call-done = f32[1792,512]{0,1:T(8,128)} async-done(((f32[1792,16]{0,1:T(8,128)}), f32[1792,512]{0,1:T(8,128)}) %all-gather.2.cloned.1.call-update) | async-done | bytes 3670032 | tf_op jit(solution)/shard_map/all_gather | solution.py:13
  171.7 8.5 %fusion = f32[1792,512]{1,0:T(8,128)S(1)} fusion(f32[1792,512]{0,1:T(8,128)} %all-gather.2.cloned.1.call-done, f32[512,512]{1,0:T(8,128)} %bitcast.7), kind=kOutput, calls=%fused_computation.1 | convolution fusion | flops 5637144576 | bytes 8388608 | tf_op jit(solution)/shard_map/dot_general | solution.py:12
  180.3 0.0 copy-start.1
  180.3 1.8 copy-done.1
  182.1 0.0 copy-done
  182.1 0.0 copy-start.2
  182.1 13.0 %fusion.1 = f32[512,448]{1,0:T(8,128)} fusion(f32[1792,512]{1,0:T(8,128)S(1)} %fusion, f32[1792,448]{0,1:T(8,128)S(1)} %copy-done), kind=kOutput, calls=%fused_computation.2 | convolution fusion | flops 4932501504 | bytes 7798784 | tf_op jit(solution)/shard_map/dot_general | solution.py:24
  195.0 0.0 reduce-scatter.2.cloned.1.call-update
  195.1 0.0 copy-done.2
  195.1 20.2 %all_gather.7 = f32[512,448]{1,0:T(8,128)S(1)} all-gather(f32[64,448]{1,0:T(8,128)S(1)} %copy-done.2), channel_id=1, replica_groups=mesh['row'=8,'col'=32] {'row'}, dimensions={0}, use_global_device_ids=true | all-gather | bytes 1032192 | tf_op jit(solution)/shard_map/all_gather | solution.py:20
  215.3 10.4 %convolution_subtract_fusion = f32[1792,448]{0,1:T(8,128)} fusion(f32[1792,448]{0,1:T(8,128)} %param.8, f32[1792,512]{1,0:T(8,128)} %copy-done.1, f32[512,448]{1,0:T(8,128)S(1)} %all_gather.7), kind=kOutput, calls=%fused_computation | convolution fusion | flops 4933304320 | bytes 11010048 | tf_op jit(solution)/shard_map/dot_general | solution.py:18
  225.7 10.7 %reduce-scatter.2.cloned.1.call-done = f32[64,448]{1,0:T(8,128)} async-done(((f32[512,448]{1,0:T(8,128)}), f32[64,448]{1,0:T(8,128)}) %reduce-scatter.2.cloned.1.call-update) | async-done | bytes 114704 | tf_op jit(solution)/shard_map/reduce_scatter | solution.py:31
Async XLA Ops:
  7.2 174.9 %copy-start = (f32[1792,448]{0,1:T(8,128)S(1)}, f32[1792,448]{0,1:T(8,128)}, u32[]{:S(2)}) copy-start(f32[1792,448]{0,1:T(8,128)} %param.9) | copy-start | bytes 9633796
  7.2 164.6 %all-gather.2.cloned.1.call-start = ((), (), s32[]{:S(2)}) async-start(), calls=%async_computation.2 | async-start | bytes 3784704 | tf_op jit(solution)/shard_map/all_gather | solution.py:13
  7.9 228.5 %reduce-scatter.2.cloned.1.call-start = ((), (), s32[]{:S(2)}) async-start(), calls=%async_computation.3 | async-start | bytes 1179648 | tf_op jit(solution)/shard_map/reduce_scatter | solution.py:31
  180.3 1.8 copy-start.1
  182.1 13.0 %copy-start.2 = (f32[64,448]{1,0:T(8,128)S(1)}, f32[64,448]{1,0:T(8,128)}, u32[]{:S(2)}) copy-start(f32[64,448]{1,0:T(8,128)} %param.7) | copy-start | bytes 344068
Sparse Core Ops, SparseCore 0:
  9.8 161.9 all-gather.1
  195.2 41.1 reduce-scatter.1
